TPU v7x, 512 devices: a whole 4x8x8 slice. The times are simulated.
512 devices in a mesh: grp: 16 (over y, core), ops: 32 (over x, z).
Axes of the slice: x: 4, y: 8, z: 8, core: 2. Of those that a mesh axis runs over, the one named last changes fastest.
Arguments:
- op_embed: bfloat16 [131072, 256], P(('grp', 'ops')), may hold values from -6 to 6
- machine_embed: bfloat16 [8192, 256], P('grp'), may hold values from -6 to 6
- cotangent: bfloat16 [131072, 256], P(('grp', 'ops')), may hold values from -6 to 6
- w_query: bfloat16 [256, 256], replicated, may hold values from -0.375 to 0.375
- w_key: bfloat16 [256, 256], replicated, may hold values from -0.375 to 0.375
- w_value: bfloat16 [256, 256], replicated, may hold values from -0.375 to 0.375
- slot_local: int32 [512, 16], P(('grp', 'ops')), may hold values from 0 to 3
- counts: int32 [131072, 16], P(('grp', 'ops')), may hold values from 0 to 128, as said below
Outputs:
- op_grad: bfloat16 [131072, 256], P(('grp', 'ops'))
- machine_grad: float32 [8192, 256], P(('grp', 'ops'))
- grad_wq: float32 [256, 256], replicated
- grad_wk: float32 [256, 256], replicated
- grad_wv: float32 [256, 256], replicated
Inputs may be any that keep to these rules, and one draw needn't show every extreme that they name: The eligible machines of slot e's block for operation o are its first counts[o, e] machines; 0 means the operation has no eligible machine in that block.
All inputs are finite; a program needn't handle non-finite values.
Results may differ from a plain program's by a relative error of at most 0.0056.
Values may be sent and summed in bfloat16 or wider, within the bound.
No kernel may reach another device: no remote copies, remote signals or barrier semaphores. Data moves between devices by JAX's collectives and lax.ppermute only.
A program may use at most 64 MiB of HBM per device.

v0:
```python
import jax
import jax.numpy as jnp
from jax import lax
from jax.sharding import PartitionSpec as P

HEADS = 8
BLK = 128
mean_scale = 0.08838834764831845


def slot_grads(queries, cotangent4, key_rows, value_rows, lengths):
    head_size = queries.shape[2]
    inv_root = head_size ** (-0.5)
    scores = (
        jnp.einsum("ohc,mhc->ohm", queries, key_rows, preferred_element_type=jnp.float32) * inv_root
    )
    sigmoid_score = jax.nn.sigmoid(scores)
    columns = lax.broadcasted_iota(jnp.int32, scores.shape, 2)
    eligible = columns < lengths[:, None, None]
    gates = jnp.where(eligible, sigmoid_score, 0.0).astype(jnp.bfloat16)
    value_dot = jnp.einsum(
        "ohc,mhc->ohm", cotangent4, value_rows, preferred_element_type=jnp.float32
    )
    dscore = jnp.where(
        eligible, mean_scale * value_dot * sigmoid_score * (1.0 - sigmoid_score) * inv_root, 0.0
    ).astype(jnp.bfloat16)
    query_part = jnp.einsum("ohm,mhc->ohc", dscore, key_rows, preferred_element_type=jnp.float32)
    key_grad = jnp.einsum(
        "ohm,ohc->mhc", dscore, queries, preferred_element_type=jnp.float32
    ).astype(jnp.bfloat16)
    value_grad = (
        mean_scale
        * jnp.einsum("ohm,ohc->mhc", gates, cotangent4, preferred_element_type=jnp.float32)
    ).astype(jnp.bfloat16)
    return (query_part, key_grad, value_grad)


def per_device(op_embed, machine_embed, cotangent, w_query, w_key, w_value, slot_local, counts):
    groups = lax.axis_size("grp")
    ops_count = op_embed.shape[0]
    model_width = op_embed.shape[1]
    head_size = model_width // HEADS
    machine_rows = machine_embed.shape[0]
    blocks_here = machine_rows // BLK
    highest = lax.Precision.HIGHEST
    both_weights = jnp.concatenate([w_key, w_value], axis=1)
    queries = jnp.dot(op_embed, w_query, preferred_element_type=jnp.float32).astype(jnp.bfloat16)
    wanted = lax.all_to_all(
        slot_local.reshape(groups, 1), "grp", split_axis=0, concat_axis=0, tiled=True
    )
    wanted_ids = wanted[:, 0]
    picker = wanted_ids[:, None] == jnp.arange(blocks_here, dtype=jnp.int32)[None, :]
    local_pairs = jnp.dot(machine_embed, both_weights, preferred_element_type=jnp.float32).astype(
        jnp.bfloat16
    )
    outgoing = local_pairs.reshape(blocks_here, BLK, 2 * model_width)[wanted_ids]
    fetched = lax.all_to_all(outgoing, "grp", split_axis=0, concat_axis=0, tiled=True)
    key_slots = fetched[:, :, :model_width].reshape(groups, BLK, HEADS, head_size)
    value_slots = fetched[:, :, model_width:].reshape(groups, BLK, HEADS, head_size)
    query_heads = queries.reshape(ops_count, HEADS, head_size)
    cot_heads = cotangent.reshape(ops_count, HEADS, head_size)

    def per_slot(summed_q, pieces):
        key_rows, value_rows, lengths = pieces
        query_part, key_grad, value_grad = slot_grads(
            query_heads, cot_heads, key_rows, value_rows, lengths
        )
        return (
            summed_q + query_part,
            (key_grad.reshape(BLK, model_width), value_grad.reshape(BLK, model_width)),
        )

    start_q = jnp.zeros((ops_count, HEADS, head_size), jnp.float32)
    summed_q, (key_grads, value_grads) = lax.scan(
        per_slot, start_q, (key_slots, value_slots, counts.T)
    )
    grad_query = summed_q.astype(jnp.bfloat16).reshape(ops_count, model_width)
    op_grad = (
        cotangent.astype(jnp.float32)
        + jnp.dot(grad_query, w_query.T, preferred_element_type=jnp.float32)
    ).astype(jnp.bfloat16)
    wq_term = jnp.einsum("od,oe->de", op_embed, grad_query, preferred_element_type=jnp.float32)
    returned = lax.all_to_all(
        jnp.concatenate([key_grads, value_grads], axis=2),
        "grp",
        split_axis=0,
        concat_axis=0,
        tiled=True,
    )
    summed = jnp.einsum(
        "gb,gr->br",
        picker.astype(jnp.bfloat16),
        returned.reshape(groups, BLK * 2 * model_width),
        preferred_element_type=jnp.float32,
    )
    summed = summed.reshape(machine_rows, 2 * model_width)
    key_total = summed[:, :model_width]
    value_total = summed[:, model_width:]
    machine_part = jnp.dot(key_total, w_key.astype(jnp.float32).T, precision=highest) + jnp.dot(
        value_total, w_value.astype(jnp.float32).T, precision=highest
    )
    embed_f = machine_embed.astype(jnp.float32)
    wk_term = jnp.dot(embed_f.T, key_total, precision=highest)
    wv_term = jnp.dot(embed_f.T, value_total, precision=highest)
    summed_total = lax.psum(machine_part, "ops")
    share_rows = machine_rows // lax.axis_size("ops")
    first_row = lax.axis_index("ops") * share_rows
    machine_grad = lax.dynamic_slice_in_dim(summed_total, first_row, share_rows, 0)
    weight_sums = lax.psum((wq_term, wk_term, wv_term), ("grp", "ops"))
    shard_count = float(groups * lax.axis_size("ops"))
    grad_wq = weight_sums[0] / shard_count
    grad_wk = weight_sums[1] / shard_count
    grad_wv = weight_sums[2] / shard_count
    return (op_grad, machine_grad, grad_wq, grad_wk, grad_wv)


def solution(mesh):
    return jax.shard_map(
        per_device,
        mesh=mesh,
        in_specs=(
            P(("grp", "ops"), None),
            P("grp", None),
            P(("grp", "ops"), None),
            P(),
            P(),
            P(),
            P(("grp", "ops"), None),
            P(("grp", "ops"), None),
        ),
        out_specs=(P(("grp", "ops"), None), P(("grp", "ops"), None), P(), P(), P()),
        check_vma=False,
    )
```

profile of v0, /device:TPU:8, one launch (start us, length us, event | category | flops | bytes accessed | tf_op | source)
XLA Modules:
  0.0 657.2 jit_solution(9235457132968034616)
XLA Ops:
  7.2 1.4 copy.46
  8.6 9.1 %all-to-all-start = ((s32[16,1,1]{2,1,0:T(1,128)}), s32[16,1,1]{2,1,0:T(1,128)S(1)}, u32[]{:S(2)}, u32[]{:S(2)}) async-start(s32[16,1,1]{2,1,0:T(1,128)} %copy.46), calls=%async_computation | async-start | bytes 16384 | tf_op jit(solution)/shard_map/all_to_all | solution.py:48
  18.9 4.9 all-to-all-done
  24.2 2.0 gather_fusion
  26.2 5.1 all-to-all-start.1
  31.7 46.8 %all-to-all-done.1 = bf16[16,128,512]{2,1,0:T(8,128)(2,1)S(1)} async-done(((bf16[16,128,512]{2,1,0:T(8,128)(2,1)}), bf16[16,128,512]{2,1,0:T(8,128)(2,1)S(1)}, u32[]{:S(2)}, u32[]{:S(2)}) %all-to-all-start.1) | async-done | bytes 2097184 | tf_op jit(solution)/shard_map/all_to_all | solution.py:57
  78.6 1.6 fusion.38
  80.2 1.7 copy.47
  81.9 1.3 copy.48
  83.2 63.6 %while.15 = (s32[]{:T(128)}, f32[256,8,32]{0,2,1:T(8,128)S(1)}, bf16[16,128,256]{1,2,0:T(8,128)(2,1)}, bf16[16,128,256]{1,2,0:T(8,128)(2,1)}, bf16[16,128,8,32]{...) while((s32[]{:T(128)}, f32[256,8,32]{0,2,1:T(8,128)S(1)}, ...), condition=%wide.region_1.2_spmd.clone, body=%wide.region_0.1_spmd.clone.sunk | while | flops 87785472 | bytes 6361235 | solution.py:74
  84.4 1.3 fusion.80
  88.4 1.3 fusion.80
  92.4 1.3 fusion.80
  96.3 1.3 fusion.80
  100.3 1.3 fusion.80
  104.3 1.3 fusion.80
  108.2 1.3 fusion.80
  112.2 1.3 fusion.80
  116.2 1.3 fusion.80
  120.2 1.3 fusion.80
  124.1 1.3 fusion.80
  128.1 1.3 fusion.80
  132.1 1.3 fusion.80
  140.1 1.3 fusion.80
  144.0 1.3 fusion.80
  146.8 3.1 pad_maximum_fusion
  149.9 6.9 %all-to-all-start.2 = ((bf16[16,128,512]{1,2,0:T(8,128)(2,1)}), bf16[16,128,512]{1,2,0:T(8,128)(2,1)}, u32[]{:S(2)}, u32[]{:S(2)}) async-start(bf16[16,128,512]{1,2,0:T(8,128)(2,1)} %pad_maximum_fusion), calls=%async_computation.2 | async-start | bytes 4194304 | tf_op jit(solution)/shard_map/all_to_all | solution.py:83
  157.7 46.3 %all-to-all-done.2 = bf16[16,128,512]{1,2,0:T(8,128)(2,1)} async-done(((bf16[16,128,512]{1,2,0:T(8,128)(2,1)}), bf16[16,128,512]{1,2,0:T(8,128)(2,1)}, u32[]{:S(2)}, u32[]{:S(2)}) %all-to-all-start.2) | async-done | bytes 2097184 | tf_op jit(solution)/shard_map/all_to_all | solution.py:83
  204.0 3.4 copy.57
  214.0 274.6 %all-reduce.6.cloned.1.call-done = (f32[256,256]{0,1:T(8,128)}, f32[256,256]{0,1:T(8,128)}, f32[256,256]{0,1:T(8,128)}) async-done(((f32[256,256]{0,1:T(8,128)}, f32[256,256]{0,1:T(8,128)}, f32[256,256]{0,1:T(8,128)}), (f32[256,256]{0,1:T(8,128)}, f32[256,256]{0,1:T(8,128)}, f32[256,256]{0,1:T(8,128)})) %all-reduce.6.cloned.1.call-update) | async-done | bytes 786448 | tf_op jit(solution)/shard_map/psum | solution.py:109
  493.2 155.8 %all-reduce.4.cloned.1.call-done = f32[512,256]{1,0:T(8,128)} async-done(((f32[512,256]{1,0:T(8,128)}), f32[512,256]{1,0:T(8,128)}) %all-reduce.4.cloned.1.call-update) | async-done | bytes 524304 | tf_op jit(solution)/shard_map/psum | solution.py:105
  649.0 1.3 constant_dynamic-slice_fusion.1
  (144 shorter events, 57.5 us)
Async XLA Ops:
  7.2 10.5 %copy-start = (bf16[512,256]{1,0:T(8,128)(2,1)S(1)}, bf16[512,256]{1,0:T(8,128)(2,1)}, u32[]{:S(2)}) copy-start(bf16[512,256]{1,0:T(8,128)(2,1)} %param.11) | copy-start | bytes 786436
  8.6 15.3 %all-to-all-start = ((s32[16,1,1]{2,1,0:T(1,128)}), s32[16,1,1]{2,1,0:T(1,128)S(1)}, u32[]{:S(2)}, u32[]{:S(2)}) async-start(s32[16,1,1]{2,1,0:T(1,128)} %copy.46), calls=%async_computation | async-start | bytes 16384 | tf_op jit(solution)/shard_map/all_to_all | solution.py:48
  26.2 5.1 copy-start.6
  26.2 5.3 copy-start.2
  26.2 5.3 copy-start.4
  26.2 52.3 %all-to-all-start.1 = ((bf16[16,128,512]{2,1,0:T(8,128)(2,1)}), bf16[16,128,512]{2,1,0:T(8,128)(2,1)S(1)}, u32[]{:S(2)}, u32[]{:S(2)}) async-start(bf16[16,128,512]{2,1,0:T(8,128)(2,1)} %gather_fusion), calls=%async_computation.1 | async-start | bytes 4194304 | tf_op jit(solution)/shard_map/all_to_all | solution.py:57
  80.2 1.7 copy-start.1
  149.9 6.9 %copy-start.3 = (bf16[256,256]{1,0:T(8,128)(2,1)S(1)}, bf16[256,256]{1,0:T(8,128)(2,1)}, u32[]{:S(2)}) copy-start(bf16[256,256]{1,0:T(8,128)(2,1)} %param.10) | copy-start | bytes 393220
  149.9 54.2 %all-to-all-start.2 = ((bf16[16,128,512]{1,2,0:T(8,128)(2,1)}), bf16[16,128,512]{1,2,0:T(8,128)(2,1)}, u32[]{:S(2)}, u32[]{:S(2)}) async-start(bf16[16,128,512]{1,2,0:T(8,128)(2,1)} %pad_maximum_fusion), calls=%async_computation.2 | async-start | bytes 4194304 | tf_op jit(solution)/shard_map/all_to_all | solution.py:83
  156.8 331.9 %all-reduce.6.cloned.1.call-start = ((), (), s32[]{:S(2)}) async-start(), calls=%async_computation.4 | async-start | bytes 1572864 | tf_op jit(solution)/shard_map/psum | solution.py:109
  208.0 3.4 copy-start.8
  208.7 3.1 copy-start.9
  211.3 1.8 copy-start.5
  211.3 1.8 copy-start.7
  211.4 437.6 %all-reduce.4.cloned.1.call-start = ((), (), s32[]{:S(2)}) async-start(), calls=%async_computation.3 | async-start | bytes 1048576 | tf_op jit(solution)/shard_map/psum | solution.py:105
Sparse Core Ops, SparseCore 0:
  211.5 277.0 all-reduce.5
  492.0 156.9 all-reduce.3
where the time goes:
time: 659 us; the launch traced here: 657 us
  waiting for transfers between devices  529 us (80%)
  matrix products  48.8 us (7%)
  local copies, waits for them, and re-layouts  38.4 us (6%)
  starting transfers between devices  21.1 us (3%)
  between operations  14.3 us (2%)
    psum x1, waiting for transfers between devices, per_device(): weight_sums = lax.psum((wq_term, wk_term, wv_term), ('grp', 'ops'))  275 us
    psum x1, waiting for transfers between devices, per_device(): summed_total = lax.psum(machine_part, 'ops')  156 us
    all_to_all x1, waiting for transfers between devices, per_device(): lax.all_to_all(outgoing, 'grp', split_axis=0, concat_axis=0, tiled=True)  46.8 us
    all_to_all x1, waiting for transfers between devices, per_device(): lax.all_to_all(jnp.concatenate([key_grads, value_grads], axis=2), 'grp',...  46.3 us
    dot_general x16, matrix products, slot_grads(): jnp.einsum('ohc,mhc->ohm', cotangent4, value_rows, preferred_element_type...  20.9 us
  transfers between devices with their start and end apart: 5, of which 5 were waited for; matrix products, arithmetic and copies ran while one was open for 1% of the time, Pallas kernels for 0%

commit v1 on v0

--- a/solution.py
+++ b/solution.py
@@ -106,7 +106,9 @@
     share_rows = machine_rows // lax.axis_size("ops")
     first_row = lax.axis_index("ops") * share_rows
     machine_grad = lax.dynamic_slice_in_dim(summed_total, first_row, share_rows, 0)
-    weight_sums = lax.psum((wq_term, wk_term, wv_term), ("grp", "ops"))
+    weight_sums = (wq_term, wk_term, wv_term)
+    for axis in ("grp", "ops"):
+        weight_sums = lax.psum(weight_sums, axis)
     shard_count = float(groups * lax.axis_size("ops"))
     grad_wq = weight_sums[0] / shard_count
     grad_wk = weight_sums[1] / shard_count

time: 659 us -> 527 us (0.80)
  waiting for transfers between devices: 529 us -> 383 us
  matrix products: 48.8 us -> 62.4 us
    psum x1, waiting for transfers between devices: 275 us -> 116 us  [per_device(): weight_sums = lax.psum(weight_sums, axis)]
    dot_general x16, matrix products: 3.44 us -> 16.9 us  [slot_grads(): jnp.einsum('ohm,mhc->ohc', dscore, key_rows, preferred_element_type=jnp.f...]
    dot_general x16, matrix products: 7.87 us -> 21.3 us  [slot_grads(): jnp.einsum('ohc,mhc->ohm', queries, key_rows, preferred_element_type=jnp....]
    dot_general x16, matrix products: 20.9 us -> 7.52 us  [slot_grads(): jnp.einsum('ohc,mhc->ohm', cotangent4, value_rows, preferred_element_type...]
    psum x1, waiting for transfers between devices: 156 us -> 169 us  [per_device(): summed_total = lax.psum(machine_part, 'ops')]
where the time goes in v1:
time: 527 us; the launch traced here: 525 us
  waiting for transfers between devices  383 us (73%)
  matrix products  62.4 us (12%)
  local copies, waits for them, and re-layouts  37.4 us (7%)
  starting transfers between devices  21.7 us (4%)
  between operations  14.3 us (3%)
  other arithmetic  5.53 us (1%)
    psum x1, waiting for transfers between devices, per_device(): summed_total = lax.psum(machine_part, 'ops')  169 us
    psum x1, waiting for transfers between devices, per_device(): weight_sums = lax.psum(weight_sums, axis)  116 us
    all_to_all x1, waiting for transfers between devices, per_device(): lax.all_to_all(outgoing, 'grp', split_axis=0, concat_axis=0, tiled=True)  46.9 us
    all_to_all x1, waiting for transfers between devices, per_device(): lax.all_to_all(jnp.concatenate([key_grads, value_grads], axis=2), 'grp',...  46.3 us
    dot_general x16, matrix products, slot_grads(): jnp.einsum('ohc,mhc->ohm', queries, key_rows, preferred_element_type=jnp....  21.3 us
    dot_general x16, matrix products, slot_grads(): jnp.einsum('ohm,mhc->ohc', dscore, key_rows, preferred_element_type=jnp.f...  16.9 us
    dynamic_slice x16, local copies, waits for them, and re-layouts, per_device(): lax.scan(per_slot, start_q, (key_slots, value_slots, counts.T))  11.3 us
    dynamic_update_slice x16, local copies, waits for them, and re-layouts, per_device(): lax.scan(per_slot, start_q, (key_slots, value_slots, counts.T))  11 us
  transfers between devices with their start and end apart: 5, of which 5 were waited for; matrix products, arithmetic and copies ran while one was open for 1% of the time, Pallas kernels for 0%

profile of v1, /device:TPU:8, one launch (start us, length us, event | category | flops | bytes accessed | tf_op | source)
XLA Modules:
  0.0 524.8 jit_solution(10441471081754524153)
XLA Ops:
  7.2 1.4 copy.46
  8.6 9.1 %all-to-all-start = ((s32[16,1,1]{2,1,0:T(1,128)}), s32[16,1,1]{2,1,0:T(1,128)S(1)}, u32[]{:S(2)}, u32[]{:S(2)}) async-start(s32[16,1,1]{2,1,0:T(1,128)} %copy.46), calls=%async_computation | async-start | bytes 16384 | tf_op jit(solution)/shard_map/all_to_all | solution.py:48
  18.9 4.9 all-to-all-done
  24.2 2.0 gather_fusion
  26.2 5.8 %all-to-all-start.1 = ((bf16[16,128,512]{2,1,0:T(8,128)(2,1)}), bf16[16,128,512]{2,1,0:T(8,128)(2,1)}, u32[]{:S(2)}, u32[]{:S(2)}) async-start(bf16[16,128,512]{2,1,0:T(8,128)(2,1)} %gather_fusion), calls=%async_computation.1 | async-start | bytes 4194304 | tf_op jit(solution)/shard_map/all_to_all | solution.py:57
  32.4 46.9 %all-to-all-done.1 = bf16[16,128,512]{2,1,0:T(8,128)(2,1)} async-done(((bf16[16,128,512]{2,1,0:T(8,128)(2,1)}), bf16[16,128,512]{2,1,0:T(8,128)(2,1)}, u32[]{:S(2)}, u32[]{:S(2)}) %all-to-all-start.1) | async-done | bytes 2097184 | tf_op jit(solution)/shard_map/all_to_all | solution.py:57
  79.3 1.7 fusion.38
  81.0 1.3 copy.47
  83.0 77.1 %while.15 = (s32[]{:T(128)}, f32[256,8,32]{0,2,1:T(8,128)S(1)}, bf16[16,128,256]{1,2,0:T(8,128)(2,1)}, bf16[16,128,256]{1,2,0:T(8,128)(2,1)}, bf16[16,128,8,32]{...) while((s32[]{:T(128)}, f32[256,8,32]{0,2,1:T(8,128)S(1)}, ...), condition=%wide.region_1.2_spmd.clone, body=%wide.region_0.1_spmd.clone.sunk | while | flops 87785472 | bytes 6361235 | solution.py:74
  83.0 1.3 fusion.79
  87.8 1.3 fusion.79
  92.6 1.3 fusion.79
  97.4 1.3 fusion.79
  102.3 1.3 fusion.79
  107.1 1.3 fusion.79
  111.9 1.3 fusion.79
  116.7 1.3 fusion.79
  121.5 1.3 fusion.79
  126.4 1.3 fusion.79
  131.2 1.3 fusion.79
  136.0 1.3 fusion.79
  140.8 1.3 fusion.79
  145.6 1.3 fusion.79
  150.5 1.3 fusion.79
  155.3 1.3 fusion.79
  160.1 3.1 pad_maximum_fusion
  163.2 6.7 %all-to-all-start.2 = ((bf16[16,128,512]{1,2,0:T(8,128)(2,1)}), bf16[16,128,512]{1,2,0:T(8,128)(2,1)}, u32[]{:S(2)}, u32[]{:S(2)}) async-start(bf16[16,128,512]{1,2,0:T(8,128)(2,1)} %pad_maximum_fusion), calls=%async_computation.2 | async-start | bytes 4194304 | tf_op jit(solution)/shard_map/all_to_all | solution.py:83
  170.9 46.3 %all-to-all-done.2 = bf16[16,128,512]{1,2,0:T(8,128)(2,1)} async-done(((bf16[16,128,512]{1,2,0:T(8,128)(2,1)}), bf16[16,128,512]{1,2,0:T(8,128)(2,1)}, u32[]{:S(2)}, u32[]{:S(2)}) %all-to-all-start.2) | async-done | bytes 2097184 | tf_op jit(solution)/shard_map/all_to_all | solution.py:83
  217.2 3.4 copy.57
  226.3 116.0 %all-reduce.7.cloned.1.call-done = (f32[256,256]{0,1:T(8,128)}, f32[256,256]{0,1:T(8,128)}, f32[256,256]{0,1:T(8,128)}) async-done(((f32[256,256]{0,1:T(8,128)}, f32[256,256]{0,1:T(8,128)}, f32[256,256]{0,1:T(8,128)}), (f32[256,256]{0,1:T(8,128)}, f32[256,256]{0,1:T(8,128)}, f32[256,256]{0,1:T(8,128)})) %all-reduce.7.cloned.1.call-update) | async-done | bytes 786448 | tf_op jit(solution)/shard_map/psum | solution.py:111
  343.2 168.9 %all-reduce.5.cloned.1.call-done = (f32[512,256]{1,0:T(8,128)}, f32[256,256]{0,1:T(8,128)}, f32[256,256]{0,1:T(8,128)}, f32[256,256]{0,1:T(8,128)}) async-done(((f32[512,256]{1,0:T(8,128)}, f32[256,256]{0,1:T(8,128)}, f32[256,256]{0,1:T(8,128)}, f32[256,256]{0,1:T(8,128)}), (f32[512,256]{1,0:T(8,128)}, f32[256,256]{0,1:T(8,128)}, f32[256,256]{0,1:T(8,128)}, ...) | async-done | bytes 1310736 | tf_op jit(solution)/shard_map/psum | solution.py:105
  516.6 1.3 constant_dynamic-slice_fusion.1
  (140 shorter events, 70.0 us)
Async XLA Ops:
  7.2 10.5 %copy-start = (bf16[512,256]{1,0:T(8,128)(2,1)S(1)}, bf16[512,256]{1,0:T(8,128)(2,1)}, u32[]{:S(2)}) copy-start(bf16[512,256]{1,0:T(8,128)(2,1)} %param.11) | copy-start | bytes 786436
  8.6 15.3 %all-to-all-start = ((s32[16,1,1]{2,1,0:T(1,128)}), s32[16,1,1]{2,1,0:T(1,128)S(1)}, u32[]{:S(2)}, u32[]{:S(2)}) async-start(s32[16,1,1]{2,1,0:T(1,128)} %copy.46), calls=%async_computation | async-start | bytes 16384 | tf_op jit(solution)/shard_map/all_to_all | solution.py:48
  26.2 5.8 %copy-start.4 = (bf16[256,256]{1,0:T(8,128)(2,1)S(1)}, bf16[256,256]{1,0:T(8,128)(2,1)}, u32[]{:S(2)}) copy-start(bf16[256,256]{1,0:T(8,128)(2,1)} %param.12) | copy-start | bytes 393220
  26.2 5.9 %copy-start.1 = (bf16[256,256]{1,0:T(8,128)(2,1)S(1)}, bf16[256,256]{1,0:T(8,128)(2,1)}, u32[]{:S(2)}) copy-start(bf16[256,256]{1,0:T(8,128)(2,1)} %param.10) | copy-start | bytes 393220
  26.2 5.9 %copy-start.2 = (bf16[256,256]{1,0:T(8,128)(2,1)S(1)}, bf16[256,256]{1,0:T(8,128)(2,1)}, u32[]{:S(2)}) copy-start(bf16[256,256]{1,0:T(8,128)(2,1)} %param.13) | copy-start | bytes 393220
  26.2 53.1 %all-to-all-start.1 = ((bf16[16,128,512]{2,1,0:T(8,128)(2,1)}), bf16[16,128,512]{2,1,0:T(8,128)(2,1)}, u32[]{:S(2)}, u32[]{:S(2)}) async-start(bf16[16,128,512]{2,1,0:T(8,128)(2,1)} %gather_fusion), calls=%async_computation.1 | async-start | bytes 4194304 | tf_op jit(solution)/shard_map/all_to_all | solution.py:57
  163.2 54.0 %all-to-all-start.2 = ((bf16[16,128,512]{1,2,0:T(8,128)(2,1)}), bf16[16,128,512]{1,2,0:T(8,128)(2,1)}, u32[]{:S(2)}, u32[]{:S(2)}) async-start(bf16[16,128,512]{1,2,0:T(8,128)(2,1)} %pad_maximum_fusion), calls=%async_computation.2 | async-start | bytes 4194304 | tf_op jit(solution)/shard_map/all_to_all | solution.py:83
  169.9 172.3 %all-reduce.7.cloned.1.call-start = ((), (), s32[]{:S(2)}) async-start(), calls=%async_computation.4 | async-start | bytes 1572864 | tf_op jit(solution)/shard_map/psum | solution.py:111
  221.2 3.4 copy-start.6
  221.9 3.1 copy-start.7
  224.5 117.8 %copy-start.3 = (bf16[256,256]{1,0:T(8,128)(2,1)S(1)}, bf16[256,256]{1,0:T(8,128)(2,1)}, u32[]{:S(2)}) copy-start(bf16[256,256]{1,0:T(8,128)(2,1)} %param.13) | copy-start | bytes 393220
  224.5 117.8 %copy-start.5 = (bf16[256,256]{1,0:T(8,128)(2,1)S(1)}, bf16[256,256]{1,0:T(8,128)(2,1)}, u32[]{:S(2)}) copy-start(bf16[256,256]{1,0:T(8,128)(2,1)} %param.12) | copy-start | bytes 393220
  224.6 287.5 %all-reduce.5.cloned.1.call-start = ((), (), s32[]{:S(2)}) async-start(), calls=%async_computation.3 | async-start | bytes 2621440 | tf_op jit(solution)/shard_map/psum | solution.py:105
Sparse Core Ops, SparseCore 0:
  224.7 117.5 all-reduce.6
  346.1 165.9 all-reduce.4
